TPU v7x, 32 devices: a whole 2x2x4 slice. The times are simulated.
32 devices in a mesh: col: 8 (over y, x, core), row: 4 (over z).
Axes of the slice: x: 2, y: 2, z: 4, core: 2. Of those that a mesh axis runs over, the one named last changes fastest.
Arguments:
- matrix: float32 [16, 512, 4096], P(None, 'row', 'col'), may hold values from -0.4 to 2.4, as said below
- pivots: int32 [8, 512], replicated, may hold values from 0 to 511, as said below
- seeds: float32 [8, 512, 512], P('col'), may hold values from -1 to 2, as said below
Outputs:
- factors: float32 [16, 512, 4096], P(None, 'row', 'col')
Inputs may be any that keep to these rules, and one draw needn't show every extreme that they name: Each row of pivots is an ordering of 0 .. 511. Block (r, j) of matrix is zero where r and j differ by more than 8. seeds[k] approximates the inverse of block (k, k) of matrix after the replacement of rows by pivots[k].
All inputs are finite; a program needn't handle non-finite values.
Results may differ from a plain program's by a relative error of at most 0.0001.
Values sent between devices are 32-bit elements; how exact they have to be, the bound alone decides.
A program may use at most 64 MiB of HBM per device.

v0:
```python
import functools

import jax
import jax.numpy as jnp
from jax import lax
from jax.experimental import pallas as pl
from jax.experimental.pallas import tpu as pltpu
from jax.sharding import PartitionSpec as P

HB = 8
F32 = jnp.float32
BF16 = jnp.bfloat16
MESH = pl.DeviceIdType.MESH


def split(x):
    high = x.astype(BF16)
    return high, (x - high.astype(F32)).astype(BF16)


def dot(left, right):
    return jnp.dot(left, right, preferred_element_type=F32)


def dot3(left, right):
    return dot(left[0], right[0]) + (dot(left[0], right[1]) + dot(left[1], right[0]))


def split3(x):
    high = x.astype(BF16)
    rest = x - high.astype(F32)
    middle = rest.astype(BF16)
    return high, middle, (rest - middle.astype(F32)).astype(BF16)


def kernel(
    ncol, nrow, a_hbm, piv_ref, seed_ref, out_ref,
    upper, mult, u_high, u_low, approx, x_high, x_low, e_high, e_low, f_high, f_low,
    usend, urecv, msend, mrecv, lsem,
):
    square = ncol == 8 and nrow == 4 and HB >= ncol - 1
    col = lax.axis_index("col")
    row = lax.axis_index("row")
    share, width = out_ref.shape[1], out_ref.shape[2]
    first = jnp.maximum(col - HB, 0)
    chip, core = col // 2, lax.rem(col, 2)

    load = pltpu.make_async_copy(a_hbm, out_ref, lsem)
    load.start()
    barrier = pltpu.get_barrier_semaphore()
    for step in range(1, nrow):
        pl.semaphore_signal(
            barrier, inc=1, device_id=(col, lax.rem(row + step, nrow)), device_id_type=MESH
        )
    for step in range(1, ncol):
        pl.semaphore_signal(
            barrier, inc=1, device_id=(lax.rem(col + step, ncol), row), device_id_type=MESH
        )
    pl.semaphore_wait(barrier, nrow + ncol - 2)
    load.wait()

    def share_copy(k, slot, source, target):
        return pltpu.make_async_remote_copy(
            src_ref=upper.at[k, source],
            dst_ref=upper.at[k, source],
            send_sem=usend.at[k, slot],
            recv_sem=urecv.at[k, source],
            device_id=(col, target),
            device_id_type=MESH,
        )

    def own_sends(k, act):
        if not square:
            for step in range(1, nrow):
                act(share_copy(k, step, row, lax.rem(row + step, nrow)))
            return
        end = (row == 0) | (row == 3)
        ahead = jnp.where(row < 2, 1, -1)

        @pl.when(end)
        def _():
            for step in (3, 2, 1):
                act(share_copy(k, step, row, row + ahead * step))

        @pl.when(~end)
        def _():
            act(share_copy(k, 1, row, row + ahead))
            act(share_copy(k, 2, row, row - ahead))

    def relayed(k):
        ahead = jnp.where(row < 2, 1, -1)
        return share_copy(k, 3, row + ahead, row - ahead)

    def start_gather(k):
        upper[k, row] = out_ref[k]
        own_sends(k, lambda copy: copy.start())

    def wait_share(k, source):
        share_copy(k, 0, source, source).wait_recv()

    def relay(k):
        if square:
            @pl.when((row == 1) | (row == 2))
            def _():
                wait_share(k, jnp.where(row < 2, row + 1, row - 1))
                relayed(k).start()

    def sources():
        if not square:
            return [(None, lax.rem(row + step, nrow)) for step in range(1, nrow)]
        end = (row == 0) | (row == 3)
        ahead = jnp.where(row < 2, 1, -1)
        return [
            (None, jnp.where(end, row + 3 * ahead, row - ahead)),
            (None, jnp.where(end, row + ahead, row + 2 * ahead)),
            (end, row + 2 * ahead),
        ]

    def finish_gather(k):
        for when, source in sources():
            if when is None:
                wait_share(k, source)
            else:
                pl.when(when)(lambda source=source: wait_share(k, source))

    def mult_copy(k, c, slot, target):
        return pltpu.make_async_remote_copy(
            src_ref=mult.at[k, c],
            dst_ref=mult.at[k, c],
            send_sem=msend.at[k, c, slot],
            recv_sem=mrecv.at[k, c],
            device_id=(target, row),
            device_id_type=MESH,
        )

    def forward(k, c, act):
        if not square:
            @pl.when((col + 1 < ncol) & (col + 1 <= k + HB))
            def _():
                act(mult_copy(k, c, 0, col + 1))

            return
        owner = k // 2
        mine = k == col
        odd = lax.rem(c, 2) == 1
        late = odd & (c > 1)
        leads = ~mine & (core == 0)
        near = owner == 0
        along_y = (mine & (chip < 2)) | (leads & near & (chip == 1) & ~odd)
        along_x = (mine & ((chip == 0) | (chip == 2))) | (
            leads & ((near & odd & (chip == 2)) | ((owner == 1) & late & (chip == 3)))
        )
        across = mine & (chip == 1) & ~late

        @pl.when(core == 0)
        def _():
            act(mult_copy(k, c, 0, col + 1))

        @pl.when(along_x | across)
        def _():
            other = jnp.where(across, 2, chip + 1 - 2 * lax.rem(chip, 2))
            act(mult_copy(k, c, 1, 2 * other))

        @pl.when(along_y)
        def _():
            act(mult_copy(k, c, 2, 2 * (chip + 2)))

    def start(copy):
        copy.start()

    def one_hot(k):
        ordering = jnp.broadcast_to(piv_ref[pl.ds(k, 1), :], (width, width))
        hits = lax.broadcasted_iota(jnp.int32, (width, width), 0) == ordering
        return jnp.where(hits, 1.0, 0.0).astype(BF16)

    def store_swapped(k):
        ordering = piv_ref[pl.ds(k, 1), :]
        mine = ordering[:, :share]
        for other in range(1, nrow):
            mine = jnp.where(row == other, ordering[:, other * share:(other + 1) * share], mine)
        hits = lax.broadcasted_iota(jnp.int32, (width, share), 0) == jnp.broadcast_to(mine, (width, share))
        hits = jnp.where(hits, 1.0, 0.0).astype(BF16)
        parts = split3(upper[k].reshape(width, width))
        contract = (((0,), (0,)), ((), ()))
        pick = lambda part: lax.dot_general(hits, part, contract, preferred_element_type=F32)
        out_ref[k] = pick(parts[0]) + (pick(parts[1]) + pick(parts[2]))

    def split_upper(k):
        high, low = split(upper[k].reshape(width, width))
        u_high[k] = high
        u_low[k] = low

    def chunk(k, c):
        mult_copy(k, c, 0, col).wait_recv()
        forward(k, c, start)
        change = dot3(split(mult[k, c]), (u_high[k], u_low[k]))
        out_ref[k + 1 + c] = out_ref[k + 1 + c] - change

    start_gather(first)

    scatter = one_hot(col)
    seed_parts = split3(seed_ref[0])
    contract = (((1,), (1,)), ((), ()))
    total = lax.dot_general(seed_parts[2], scatter, contract, preferred_element_type=F32)
    total += lax.dot_general(seed_parts[1], scatter, contract, preferred_element_type=F32)
    total += lax.dot_general(seed_parts[0], scatter, contract, preferred_element_type=F32)
    approx[...] = total
    high, low = split(total)
    x_high[...] = high
    x_low[...] = low
    relay(first)

    def update(k, carry):
        finish_gather(k)
        split_upper(k)

        @pl.when(k > first)
        def _():
            chunk(k - 1, 1)

        chunk(k, 0)
        start_gather(k + 1)

        @pl.when(k > first)
        def _():
            @pl.loop(2, HB)
            def _(c):
                chunk(k - 1, c)

        store_swapped(k)
        relay(k + 1)
        return carry

    lax.fori_loop(first, col, update, 0)

    @pl.when(col > first)
    def _():
        chunk(col - 1, 1)

    seed = (x_high[...], x_low[...])
    ahead = dot3(split(out_ref[col + 1]), seed)

    def residual(source):
        high, low = split(upper[col, source])
        rows = lax.broadcasted_iota(jnp.int32, (share, width), 0) + source * share
        unit = jnp.where(rows == lax.broadcasted_iota(jnp.int32, (share, width), 1), 1.0, 0.0)
        left = unit - dot3((high, low), (x_high[...], x_low[...]))
        high, low = split(left)
        e_high[source] = high
        e_low[source] = low

    residual(row)
    if square:
        @pl.when((row == 1) | (row == 2))
        def _():
            residual(jnp.where(row < 2, row + 1, row - 1))
    for when, source in sources():
        def arrive(source=source):
            wait_share(col, source)
            residual(source)

        if when is None:
            arrive()
        else:
            pl.when(when)(arrive)

    error = (e_high[...].reshape(width, width), e_low[...].reshape(width, width))
    high, low = split(dot3(error, error))
    f_high[...] = high
    f_low[...] = low
    ahead = ahead + dot3(split(ahead), error)
    mult[col, 0] = ahead + dot3(split(ahead), (high, low))
    forward(col, 0, start)

    better = approx[...]
    better = better + dot3((x_high[...], x_low[...]), (e_high[...].reshape(width, width), e_low[...].reshape(width, width)))
    better = better + dot3(split(better), (f_high[...], f_low[...]))
    high, low = split(better)
    x_high[...] = high
    x_low[...] = low

    @pl.loop(1, HB)
    def _(c):
        @pl.when((col > first) & (c + 1 < HB))
        def _():
            chunk(col - 1, c + 1)

        mult[col, c] = dot3(split(out_ref[col + 1 + c]), (x_high[...], x_low[...]))
        forward(col, c, start)

    store_swapped(col)
    f_high[...] = one_hot(col)

    @pl.loop(0, HB)
    def _(c):
        parts = split3(mult[col, c])
        target = f_high[...]
        out_ref[col + 1 + c] = dot(parts[0], target) + (dot(parts[1], target) + dot(parts[2], target))

    def drain(k, carry):
        own_sends(k, lambda copy: copy.wait_send())
        if square:
            @pl.when((row == 1) | (row == 2))
            def _():
                relayed(k).wait_send()

        @pl.loop(0, HB)
        def _(c):
            forward(k, c, lambda copy: copy.wait_send())

        return carry

    lax.fori_loop(first, col + 1, drain, 0)


def local(matrix, pivots, seeds):
    ncol = lax.axis_size("col")
    nrow = lax.axis_size("row")
    nblk, share, width = matrix.shape
    vmem = pl.BlockSpec(memory_space=pltpu.VMEM)
    half = pltpu.VMEM((width, width), BF16)
    return pl.pallas_call(
        functools.partial(kernel, ncol, nrow),
        out_shape=jax.ShapeDtypeStruct(matrix.shape, F32),
        in_specs=[pl.BlockSpec(memory_space=pl.ANY), vmem, vmem],
        out_specs=vmem,
        scratch_shapes=[
            pltpu.VMEM((ncol, nrow, share, width), F32),
            pltpu.VMEM((ncol, HB, share, width), F32),
            pltpu.VMEM((ncol, width, width), BF16),
            pltpu.VMEM((ncol, width, width), BF16),
            pltpu.VMEM((width, width), F32),
            half,
            half,
            pltpu.VMEM((nrow, share, width), BF16),
            pltpu.VMEM((nrow, share, width), BF16),
            half,
            half,
            pltpu.SemaphoreType.DMA((ncol, nrow)),
            pltpu.SemaphoreType.DMA((ncol, nrow)),
            pltpu.SemaphoreType.DMA((ncol, HB, 3)),
            pltpu.SemaphoreType.DMA((ncol, HB)),
            pltpu.SemaphoreType.DMA,
        ],
        compiler_params=pltpu.CompilerParams(
            collective_id=0, has_side_effects=True, vmem_limit_bytes=60 * 1024 * 1024
        ),
    )(matrix, pivots, seeds)


def solution(mesh):
    return jax.shard_map(
        local,
        mesh=mesh,
        in_specs=(P(None, "row", "col"), P(), P("col", None, None)),
        out_specs=P(None, "row", "col"),
        check_vma=False,
    )
```

profile of v0, /device:TPU:7, one launch (start us, length us, event | category | flops | bytes accessed | tf_op | source)
XLA Modules:
  0.0 236.0 jit_solution(14933428151439403033)
XLA Ops:
  0.0 231.2 %shard_map.37 = f32[16,128,512]{2,1,0:T(8,128)} custom-call(f32[16,128,512]{2,1,0:T(8,128)} %a_hbm.1, s32[8,512]{1,0:T(8,128)} %piv_ref.1, f32[1,512,512]{2,1,0:T(8,128)} %seed_ref.1), custom_call_target="tpu_custom_call" | custom-call | tf_op jit(solution)/shard_map/pallas_call | solution.py:322
  231.2 4.8 %copy.5 = f32[16,128,512]{2,1,0:T(8,128)} copy(f32[16,128,512]{2,1,0:T(8,128)} %shard_map.37) | data formatting | bytes 8388608
where the time goes:
time: 236 us
  Pallas kernels  231 us (98%)
  local copies, waits for them, and re-layouts  4.81 us (2%)
    pallas_call x1, Pallas kernels, local(): pl.pallas_call(functools.partial(kernel, ncol, nrow), out_shape=jax.Shape...  231 us
    unnamed x1, local copies, waits for them, and re-layouts  4.81 us

commit v1 on v0

--- a/solution.py
+++ b/solution.py
@@ -36,7 +36,7 @@
 def kernel(
     ncol, nrow, a_hbm, piv_ref, seed_ref, out_ref,
     upper, mult, u_high, u_low, approx, x_high, x_low, e_high, e_low, f_high, f_low,
-    usend, urecv, msend, mrecv, lsem,
+    usend, urecv, msend, mrecv, lsem, turn_sem, go_sem,
 ):
     square = ncol == 8 and nrow == 4 and HB >= ncol - 1
     col = lax.axis_index("col")
@@ -44,6 +44,11 @@
     share, width = out_ref.shape[1], out_ref.shape[2]
     first = jnp.maximum(col - HB, 0)
     chip, core = col // 2, lax.rem(col, 2)
+    early = (core == 1) if square else (col < 0)
+    busy = (col - core) if square else col
+
+    middle = HB // 2 + 1
+    holds = (core == 0) if square else (col < 0)
 
     load = pltpu.make_async_copy(a_hbm, out_ref, lsem)
     load.start()
@@ -59,6 +64,9 @@
     pl.semaphore_wait(barrier, nrow + ncol - 2)
     load.wait()
 
+    def start(copy):
+        copy.start()
+
     def share_copy(k, slot, source, target):
         return pltpu.make_async_remote_copy(
             src_ref=upper.at[k, source],
@@ -69,59 +77,64 @@
             device_id_type=MESH,
         )
 
+    end = (row == 0) | (row == 3)
+    ahead = jnp.where(row < 2, 1, -1)
+
     def own_sends(k, act):
         if not square:
             for step in range(1, nrow):
                 act(share_copy(k, step, row, lax.rem(row + step, nrow)))
             return
-        end = (row == 0) | (row == 3)
-        ahead = jnp.where(row < 2, 1, -1)
+        act(share_copy(k, 1, row, row + ahead))
+
+        @pl.when(~end)
+        def _():
+            act(share_copy(k, 2, row, row - ahead))
+
+    def second_sends(k, act):
+        if not square:
+            return
 
         @pl.when(end)
         def _():
-            for step in (3, 2, 1):
-                act(share_copy(k, step, row, row + ahead * step))
+            act(share_copy(k, 2, row, row + 3 * ahead))
+            act(share_copy(k, 3, row, row + 2 * ahead))
 
         @pl.when(~end)
         def _():
-            act(share_copy(k, 1, row, row + ahead))
-            act(share_copy(k, 2, row, row - ahead))
-
-    def relayed(k):
-        ahead = jnp.where(row < 2, 1, -1)
-        return share_copy(k, 3, row + ahead, row - ahead)
+            act(share_copy(k, 3, row + ahead, row - ahead))
 
     def start_gather(k):
         upper[k, row] = out_ref[k]
-        own_sends(k, lambda copy: copy.start())
+        own_sends(k, start)
 
     def wait_share(k, source):
         share_copy(k, 0, source, source).wait_recv()
 
     def relay(k):
         if square:
-            @pl.when((row == 1) | (row == 2))
-            def _():
-                wait_share(k, jnp.where(row < 2, row + 1, row - 1))
-                relayed(k).start()
+            wait_share(k, row + ahead)
+            @pl.when((core == 1) & (k < col))
+            def _():
+                pl.semaphore_wait(turn_sem, 1)
+
+            second_sends(k, start)
+
+    def pass_turn(k):
+        if square:
+            @pl.when(core == 0)
+            def _():
+                second_sends(k, lambda copy: copy.wait_send())
+                pl.semaphore_signal(turn_sem, inc=1, device_id=(col + 1, row), device_id_type=MESH)
 
     def sources():
         if not square:
-            return [(None, lax.rem(row + step, nrow)) for step in range(1, nrow)]
-        end = (row == 0) | (row == 3)
-        ahead = jnp.where(row < 2, 1, -1)
-        return [
-            (None, jnp.where(end, row + 3 * ahead, row - ahead)),
-            (None, jnp.where(end, row + ahead, row + 2 * ahead)),
-            (end, row + 2 * ahead),
-        ]
+            return [lax.rem(row + step, nrow) for step in range(1, nrow)]
+        return [jnp.where(end, row + 3 * ahead, row - ahead), row + 2 * ahead]
 
     def finish_gather(k):
-        for when, source in sources():
-            if when is None:
-                wait_share(k, source)
-            else:
-                pl.when(when)(lambda source=source: wait_share(k, source))
+        for source in sources():
+            wait_share(k, source)
 
     def mult_copy(k, c, slot, target):
         return pltpu.make_async_remote_copy(
@@ -133,40 +146,34 @@
             device_id_type=MESH,
         )
 
-    def forward(k, c, act):
+    def forward(k, c, act, near=True, far=True):
         if not square:
             @pl.when((col + 1 < ncol) & (col + 1 <= k + HB))
             def _():
                 act(mult_copy(k, c, 0, col + 1))
 
             return
-        owner = k // 2
         mine = k == col
-        odd = lax.rem(c, 2) == 1
-        late = odd & (c > 1)
         leads = ~mine & (core == 0)
-        near = owner == 0
-        along_y = (mine & (chip < 2)) | (leads & near & (chip == 1) & ~odd)
-        along_x = (mine & ((chip == 0) | (chip == 2))) | (
-            leads & ((near & odd & (chip == 2)) | ((owner == 1) & late & (chip == 3)))
-        )
-        across = mine & (chip == 1) & ~late
-
-        @pl.when(core == 0)
-        def _():
-            act(mult_copy(k, c, 0, col + 1))
-
-        @pl.when(along_x | across)
-        def _():
-            other = jnp.where(across, 2, chip + 1 - 2 * lax.rem(chip, 2))
-            act(mult_copy(k, c, 1, 2 * other))
-
-        @pl.when(along_y)
-        def _():
-            act(mult_copy(k, c, 2, 2 * (chip + 2)))
-
-    def start(copy):
-        copy.start()
+        first_part = (k == 0) & (c < middle)
+        along_y = (mine & (chip < 2)) | (leads & first_part & (chip == 1))
+        along_x = (mine & ((chip == 0) | (chip == 2))) | (leads & (k < 2) & ~first_part & (chip == 2))
+        across = mine & (chip == 1)
+
+        if near:
+            @pl.when(core == 0)
+            def _():
+                act(mult_copy(k, c, 0, col + 1))
+
+        if far:
+            @pl.when(along_x | across)
+            def _():
+                other = jnp.where(across, 2, chip + 1 - 2 * lax.rem(chip, 2))
+                act(mult_copy(k, c, 1, 2 * other))
+
+            @pl.when(along_y)
+            def _():
+                act(mult_copy(k, c, 2, 2 * (chip + 2)))
 
     def one_hot(k):
         ordering = jnp.broadcast_to(piv_ref[pl.ds(k, 1), :], (width, width))
@@ -196,6 +203,21 @@
         change = dot3(split(mult[k, c]), (u_high[k], u_low[k]))
         out_ref[k + 1 + c] = out_ref[k + 1 + c] - change
 
+    def drain(k, carry):
+        own_sends(k, lambda copy: copy.wait_send())
+
+        @pl.when(early)
+        def _():
+            second_sends(k, lambda copy: copy.wait_send())
+
+        @pl.loop(0, HB)
+        def _(c):
+            @pl.when(k < ncol - 1)
+            def _():
+                forward(k, c, lambda copy: copy.wait_send())
+
+        return carry
+
     start_gather(first)
 
     scatter = one_hot(col)
@@ -209,36 +231,58 @@
     x_high[...] = high
     x_low[...] = low
     relay(first)
+    pass_turn(first)
+
+    def rest(k):
+        @pl.when(k >= first)
+        def _():
+            @pl.loop(middle, HB)
+            def _(c):
+                chunk(k, c)
 
     def update(k, carry):
         finish_gather(k)
         split_upper(k)
-
-        @pl.when(k > first)
-        def _():
-            chunk(k - 1, 1)
-
         chunk(k, 0)
+
         start_gather(k + 1)
-
-        @pl.when(k > first)
+        relay(k + 1)
+        chunk(k, 1)
+        pass_turn(k + 1)
+
+        @pl.when(k + 1 < busy)
+        def _():
+            rest(k - 1)
+
+            @pl.loop(2, middle)
+            def _(c):
+                chunk(k, c)
+
+        store_swapped(k)
+        return carry
+
+    lax.fori_loop(first, col, update, 0)
+
+    @pl.when(early)
+    def _():
+        rest(col - 3)
+
+        @pl.when(col - 2 >= first)
         def _():
             @pl.loop(2, HB)
             def _(c):
-                chunk(k - 1, c)
-
-        store_swapped(k)
-        relay(k + 1)
-        return carry
-
-    lax.fori_loop(first, col, update, 0)
-
-    @pl.when(col > first)
-    def _():
-        chunk(col - 1, 1)
+                chunk(col - 2, c)
+
+        @pl.when(col > first)
+        def _():
+            @pl.loop(2, HB)
+            def _(c):
+                chunk(col - 1, c)
+
+        lax.fori_loop(first, col - 1, drain, 0)
 
     seed = (x_high[...], x_low[...])
-    ahead = dot3(split(out_ref[col + 1]), seed)
+    product = dot3(split(out_ref[col + 1]), seed)
 
     def residual(source):
         high, low = split(upper[col, source])
@@ -251,66 +295,90 @@
 
     residual(row)
     if square:
-        @pl.when((row == 1) | (row == 2))
-        def _():
-            residual(jnp.where(row < 2, row + 1, row - 1))
-    for when, source in sources():
-        def arrive(source=source):
-            wait_share(col, source)
-            residual(source)
-
-        if when is None:
-            arrive()
-        else:
-            pl.when(when)(arrive)
-
+        residual(row + ahead)
+    for source in sources():
+        wait_share(col, source)
+        residual(source)
     error = (e_high[...].reshape(width, width), e_low[...].reshape(width, width))
-    high, low = split(dot3(error, error))
-    f_high[...] = high
-    f_low[...] = low
-    ahead = ahead + dot3(split(ahead), error)
-    mult[col, 0] = ahead + dot3(split(ahead), (high, low))
+    product = product + dot3(split(product), error)
+    mult[col, 0] = product + dot3(split(dot3(split(product), error)), error)
     forward(col, 0, start)
-
-    better = approx[...]
-    better = better + dot3((x_high[...], x_low[...]), (e_high[...].reshape(width, width), e_low[...].reshape(width, width)))
-    better = better + dot3(split(better), (f_high[...], f_low[...]))
-    high, low = split(better)
-    x_high[...] = high
-    x_low[...] = low
+    if square:
+        @pl.when(core == 1)
+        def _():
+            pl.semaphore_signal(go_sem, inc=1, device_id=(col - 1, row), device_id_type=MESH)
+
+    error = (e_high[...].reshape(width, width), e_low[...].reshape(width, width))
+    better = approx[...] + dot3((x_high[...], x_low[...]), error)
+    better = better + dot3(split(better), split(dot3(error, error)))
+
+    target = one_hot(col)
+    f_high[...] = target
+
+    @pl.when(col == ncol - 1)
+    def _():
+        parts = split3(better)
+        swapped = dot(parts[0], target) + (dot(parts[1], target) + dot(parts[2], target))
+        high, low = split(swapped)
+        x_high[...] = high
+        x_low[...] = low
+
+    @pl.when(col < ncol - 1)
+    def _():
+        high, low = split(better)
+        x_high[...] = high
+        x_low[...] = low
+
+    @pl.when(~early)
+    def _():
+        rest(col - 2)
 
     @pl.loop(1, HB)
     def _(c):
-        @pl.when((col > first) & (c + 1 < HB))
+        @pl.when((col > first) & ~early & (c + 1 < HB))
         def _():
             chunk(col - 1, c + 1)
 
-        mult[col, c] = dot3(split(out_ref[col + 1 + c]), (x_high[...], x_low[...]))
-        forward(col, c, start)
+        last = dot3(split(out_ref[col + 1 + c]), (x_high[...], x_low[...]))
+
+        @pl.when(col < ncol - 1)
+        def _():
+            mult[col, c] = last
+            forward(col, c, start, far=False)
+
+            @pl.when(~holds | (c < middle))
+            def _():
+                forward(col, c, start, near=False)
+
+        @pl.when(col == ncol - 1)
+        def _():
+            out_ref[col + 1 + c] = last
 
     store_swapped(col)
-    f_high[...] = one_hot(col)
-
-    @pl.loop(0, HB)
-    def _(c):
+
+    def permute(c):
         parts = split3(mult[col, c])
         target = f_high[...]
         out_ref[col + 1 + c] = dot(parts[0], target) + (dot(parts[1], target) + dot(parts[2], target))
 
-    def drain(k, carry):
-        own_sends(k, lambda copy: copy.wait_send())
-        if square:
-            @pl.when((row == 1) | (row == 2))
-            def _():
-                relayed(k).wait_send()
-
-        @pl.loop(0, HB)
+    permute(0)
+
+    @pl.when(col < ncol - 1)
+    def _():
+        @pl.loop(1, HB)
         def _(c):
-            forward(k, c, lambda copy: copy.wait_send())
-
-        return carry
-
-    lax.fori_loop(first, col + 1, drain, 0)
+            permute(c)
+
+    if square:
+        @pl.when(core == 0)
+        def _():
+            pl.semaphore_wait(go_sem, 1)
+
+            @pl.loop(middle, HB)
+            def _(c):
+                forward(col, c, start, near=False)
+
+    lax.fori_loop(jnp.where(early, jnp.maximum(first, col - 1), first), col + 1, drain, 0)
 
 
 def local(matrix, pivots, seeds):
@@ -341,6 +409,8 @@
             pltpu.SemaphoreType.DMA((ncol, HB, 3)),
             pltpu.SemaphoreType.DMA((ncol, HB)),
             pltpu.SemaphoreType.DMA,
+            pltpu.SemaphoreType.REGULAR,
+            pltpu.SemaphoreType.REGULAR,
         ],
         compiler_params=pltpu.CompilerParams(
             collective_id=0, has_side_effects=True, vmem_limit_bytes=60 * 1024 * 1024

time: 236 us -> 222 us (0.941)
  Pallas kernels: 231 us -> 217 us
    pallas_call x1, Pallas kernels: 231 us -> 217 us  [local(): pl.pallas_call(functools.partial(kernel, ncol, nrow), out_shape=jax.Shape...]
where the time goes in v1:
time: 222 us
  Pallas kernels  217 us (98%)
  local copies, waits for them, and re-layouts  4.81 us (2%)
    pallas_call x1, Pallas kernels, local(): pl.pallas_call(functools.partial(kernel, ncol, nrow), out_shape=jax.Shape...  217 us
    unnamed x1, local copies, waits for them, and re-layouts  4.81 us

profile of v1, /device:TPU:7, one launch (start us, length us, event | category | flops | bytes accessed | tf_op | source)
XLA Modules:
  0.0 221.6 jit_solution(13393104792828057299)
XLA Ops:
  0.0 216.8 %shard_map.37 = f32[16,128,512]{2,1,0:T(8,128)} custom-call(f32[16,128,512]{2,1,0:T(8,128)} %a_hbm.1, s32[8,512]{1,0:T(8,128)} %piv_ref.1, f32[1,512,512]{2,1,0:T(8,128)} %seed_ref.1), custom_call_target="tpu_custom_call" | custom-call | tf_op jit(solution)/shard_map/pallas_call | solution.py:390
  216.8 4.8 %copy.5 = f32[16,128,512]{2,1,0:T(8,128)} copy(f32[16,128,512]{2,1,0:T(8,128)} %shard_map.37) | data formatting | bytes 8388608

commit v2 on v1

--- a/solution.py
+++ b/solution.py
@@ -49,6 +49,8 @@
 
     middle = HB // 2 + 1
     holds = (core == 0) if square else (col < 0)
+    sent_x = jnp.where(chip == 1, 2, middle)
+    thin = (chip == 2) if square else (col < 0)
 
     load = pltpu.make_async_copy(a_hbm, out_ref, lsem)
     load.start()
@@ -146,7 +148,7 @@
             device_id_type=MESH,
         )
 
-    def forward(k, c, act, near=True, far=True):
+    def forward(k, c, act, near=True, x=True, y=True):
         if not square:
             @pl.when((col + 1 < ncol) & (col + 1 <= k + HB))
             def _():
@@ -165,13 +167,14 @@
             def _():
                 act(mult_copy(k, c, 0, col + 1))
 
-        if far:
-            @pl.when(along_x | across)
+        if x is not False:
+            @pl.when((along_x | across) & x)
             def _():
                 other = jnp.where(across, 2, chip + 1 - 2 * lax.rem(chip, 2))
                 act(mult_copy(k, c, 1, 2 * other))
 
-            @pl.when(along_y)
+        if y is not False:
+            @pl.when(along_y & y)
             def _():
                 act(mult_copy(k, c, 2, 2 * (chip + 2)))
 
@@ -236,7 +239,7 @@
     def rest(k):
         @pl.when(k >= first)
         def _():
-            @pl.loop(middle, HB)
+            @pl.loop(jnp.where(thin & (k == 2), 3, middle), HB)
             def _(c):
                 chunk(k, c)
 
@@ -248,13 +251,18 @@
         start_gather(k + 1)
         relay(k + 1)
         chunk(k, 1)
+
+        @pl.when(thin & (k == 3))
+        def _():
+            chunk(k - 1, 2)
+
         pass_turn(k + 1)
 
         @pl.when(k + 1 < busy)
         def _():
             rest(k - 1)
 
-            @pl.loop(2, middle)
+            @pl.loop(2, jnp.where(thin & (k == 2), 2, middle))
             def _(c):
                 chunk(k, c)
 
@@ -344,11 +352,7 @@
         @pl.when(col < ncol - 1)
         def _():
             mult[col, c] = last
-            forward(col, c, start, far=False)
-
-            @pl.when(~holds | (c < middle))
-            def _():
-                forward(col, c, start, near=False)
+            forward(col, c, start, x=~holds | (c < sent_x), y=~holds | (c < middle))
 
         @pl.when(col == ncol - 1)
         def _():
@@ -374,9 +378,9 @@
         def _():
             pl.semaphore_wait(go_sem, 1)
 
-            @pl.loop(middle, HB)
+            @pl.loop(2, HB)
             def _(c):
-                forward(col, c, start, near=False)
+                forward(col, c, start, near=False, x=c >= sent_x, y=c >= middle)
 
     lax.fori_loop(jnp.where(early, jnp.maximum(first, col - 1), first), col + 1, drain, 0)
 
@@ -387,6 +391,8 @@
     nblk, share, width = matrix.shape
     vmem = pl.BlockSpec(memory_space=pltpu.VMEM)
     half = pltpu.VMEM((width, width), BF16)
+    words = 2 * nblk * share * width + ncol * width * width * 2 + ncol * HB * share * width + 6 * width * width
+    limit = min(4 * words + 2**20, 60 * 1024 * 1024)
     return pl.pallas_call(
         functools.partial(kernel, ncol, nrow),
         out_shape=jax.ShapeDtypeStruct(matrix.shape, F32),
@@ -413,7 +419,7 @@
             pltpu.SemaphoreType.REGULAR,
         ],
         compiler_params=pltpu.CompilerParams(
-            collective_id=0, has_side_effects=True, vmem_limit_bytes=60 * 1024 * 1024
+            collective_id=0, has_side_effects=True, vmem_limit_bytes=limit
         ),
     )(matrix, pivots, seeds)
 

time: 222 us -> 195 us (0.88)
  Pallas kernels: 217 us -> 191 us
    pallas_call x1, Pallas kernels: 217 us -> 191 us  [local(): pl.pallas_call(functools.partial(kernel, ncol, nrow), out_shape=jax.Shape...]
    unnamed x1 -> x5, local copies, waits for them, and re-layouts: 4.81 us -> 3.96 us
where the time goes in v2:
time: 195 us
  Pallas kernels  191 us (98%)
  local copies, waits for them, and re-layouts  3.96 us (2%)
    pallas_call x1, Pallas kernels, local(): pl.pallas_call(functools.partial(kernel, ncol, nrow), out_shape=jax.Shape...  191 us
    unnamed x5, local copies, waits for them, and re-layouts  3.96 us

profile of v2, /device:TPU:7, one launch (start us, length us, event | category | flops | bytes accessed | tf_op | source)
XLA Modules:
  0.0 195.1 jit_solution(14527822338333387078)
XLA Ops:
  0.0 0.0 copy-start
  0.0 1.2 copy-done
  1.2 0.0 copy-start.1
  1.2 0.7 copy-done.1
  1.9 191.2 %shard_map.37 = f32[16,128,512]{2,1,0:T(8,128)S(1)} custom-call(f32[16,128,512]{2,1,0:T(8,128)} %a_hbm.1, s32[8,512]{1,0:T(8,128)S(1)} %copy-done.1, f32[1,512,512]{2,1,0:T(8,128)S(1)} %copy-done), custom_call_target="tpu_custom_call" | custom-call | tf_op jit(solution)/shard_map/pallas_call | solution.py:396
  193.1 2.0 %copy.5 = f32[16,128,512]{2,1,0:T(8,128)} copy(f32[16,128,512]{2,1,0:T(8,128)S(1)} %shard_map.37) | data formatting | bytes 8388608
Async XLA Ops:
  0.0 1.2 copy-start
  1.2 0.7 copy-start.1

commit v3 on v2

--- a/solution.py
+++ b/solution.py
@@ -34,25 +34,26 @@
 
 
 def kernel(
-    ncol, nrow, a_hbm, piv_ref, seed_ref, out_ref,
-    upper, mult, u_high, u_low, approx, x_high, x_low, e_high, e_low, f_high, f_low,
-    usend, urecv, msend, mrecv, lsem, turn_sem, go_sem,
+    ncol, nrow, a_hbm, piv_ref, seed_ref, out_any,
+    work, upper, mult, u_high, u_low, approx, x_high, x_low, e_high, e_low, f_high, f_low,
+    usend, urecv, msend, mrecv, lsem, turn_sem, go_sem, osem,
 ):
     square = ncol == 8 and nrow == 4 and HB >= ncol - 1
     col = lax.axis_index("col")
     row = lax.axis_index("row")
-    share, width = out_ref.shape[1], out_ref.shape[2]
+    share, width = work.shape[1], work.shape[2]
     first = jnp.maximum(col - HB, 0)
     chip, core = col // 2, lax.rem(col, 2)
     early = (core == 1) if square else (col < 0)
     busy = (col - core) if square else col
+    final = early & (col == ncol - 1)
 
     middle = HB // 2 + 1
     holds = (core == 0) if square else (col < 0)
     sent_x = jnp.where(chip == 1, 2, middle)
     thin = (chip == 2) if square else (col < 0)
 
-    load = pltpu.make_async_copy(a_hbm, out_ref, lsem)
+    load = pltpu.make_async_copy(a_hbm, work, lsem)
     load.start()
     barrier = pltpu.get_barrier_semaphore()
     for step in range(1, nrow):
@@ -66,6 +67,18 @@
     pl.semaphore_wait(barrier, nrow + ncol - 2)
     load.wait()
 
+    def row_out(r):
+        return pltpu.make_async_copy(work.at[r], out_any.at[r], osem.at[r])
+
+    @pl.loop(0, first)
+    def _(r):
+        row_out(r).start()
+
+    @pl.loop(col + HB + 1, work.shape[0])
+    def _(r):
+        row_out(r).start()
+
+
     def start(copy):
         copy.start()
 
@@ -93,13 +106,14 @@
         def _():
             act(share_copy(k, 2, row, row - ahead))
 
-    def second_sends(k, act):
+    def second_sends(k, act, far=True):
         if not square:
             return
 
         @pl.when(end)
         def _():
-            act(share_copy(k, 2, row, row + 3 * ahead))
+            if far:
+                act(share_copy(k, 2, row, row + 3 * ahead))
             act(share_copy(k, 3, row, row + 2 * ahead))
 
         @pl.when(~end)
@@ -107,7 +121,7 @@
             act(share_copy(k, 3, row + ahead, row - ahead))
 
     def start_gather(k):
-        upper[k, row] = out_ref[k]
+        upper[k, row] = work[k]
         own_sends(k, start)
 
     def wait_share(k, source):
@@ -126,7 +140,10 @@
         if square:
             @pl.when(core == 0)
             def _():
-                second_sends(k, lambda copy: copy.wait_send())
+                @pl.when(end)
+                def _():
+                    share_copy(k, 2, row, row + 3 * ahead).wait_send()
+
                 pl.semaphore_signal(turn_sem, inc=1, device_id=(col + 1, row), device_id_type=MESH)
 
     def sources():
@@ -193,7 +210,8 @@
         parts = split3(upper[k].reshape(width, width))
         contract = (((0,), (0,)), ((), ()))
         pick = lambda part: lax.dot_general(hits, part, contract, preferred_element_type=F32)
-        out_ref[k] = pick(parts[0]) + (pick(parts[1]) + pick(parts[2]))
+        work[k] = pick(parts[0]) + (pick(parts[1]) + pick(parts[2]))
+        row_out(k).start()
 
     def split_upper(k):
         high, low = split(upper[k].reshape(width, width))
@@ -204,14 +222,16 @@
         mult_copy(k, c, 0, col).wait_recv()
         forward(k, c, start)
         change = dot3(split(mult[k, c]), (u_high[k], u_low[k]))
-        out_ref[k + 1 + c] = out_ref[k + 1 + c] - change
+        work[k + 1 + c] = work[k + 1 + c] - change
 
     def drain(k, carry):
         own_sends(k, lambda copy: copy.wait_send())
 
-        @pl.when(early)
-        def _():
-            second_sends(k, lambda copy: copy.wait_send())
+        second_sends(k, lambda copy: copy.wait_send(), far=False)
+
+        @pl.when(early & end)
+        def _():
+            share_copy(k, 2, row, row + 3 * ahead).wait_send()
 
         @pl.loop(0, HB)
         def _(c):
@@ -234,12 +254,15 @@
     x_high[...] = high
     x_low[...] = low
     relay(first)
-    pass_turn(first)
-
-    def rest(k):
+
+    @pl.when(first < col)
+    def _():
+        pass_turn(first)
+
+    def rest(k, skip=0):
         @pl.when(k >= first)
         def _():
-            @pl.loop(jnp.where(thin & (k == 2), 3, middle), HB)
+            @pl.loop(jnp.where(thin & (k == 2), 3 + skip, middle), HB)
             def _(c):
                 chunk(k, c)
 
@@ -256,7 +279,9 @@
         def _():
             chunk(k - 1, 2)
 
-        pass_turn(k + 1)
+        @pl.when(k + 1 < col)
+        def _():
+            pass_turn(k + 1)
 
         @pl.when(k + 1 < busy)
         def _():
@@ -271,13 +296,12 @@
 
     lax.fori_loop(first, col, update, 0)
 
-    @pl.when(early)
-    def _():
-        rest(col - 3)
+    def overdue(skip):
+        rest(col - 3, skip)
 
         @pl.when(col - 2 >= first)
         def _():
-            @pl.loop(2, HB)
+            @pl.loop(2 + skip, HB)
             def _(c):
                 chunk(col - 2, c)
 
@@ -287,10 +311,21 @@
             def _(c):
                 chunk(col - 1, c)
 
+    @pl.when(early & ~final & (col - 2 >= first))
+    def _():
+        chunk(col - 2, 2)
+
+        @pl.when(thin & (col == 5))
+        def _():
+            chunk(col - 3, 3)
+
+    @pl.when(final)
+    def _():
+        overdue(0)
         lax.fori_loop(first, col - 1, drain, 0)
 
     seed = (x_high[...], x_low[...])
-    product = dot3(split(out_ref[col + 1]), seed)
+    product = dot3(split(work[col + 1]), seed)
 
     def residual(source):
         high, low = split(upper[col, source])
@@ -304,6 +339,7 @@
     residual(row)
     if square:
         residual(row + ahead)
+    pass_turn(col)
     for source in sources():
         wait_share(col, source)
         residual(source)
@@ -341,13 +377,17 @@
     def _():
         rest(col - 2)
 
+    @pl.when(early & ~final)
+    def _():
+        overdue(1)
+
     @pl.loop(1, HB)
     def _(c):
         @pl.when((col > first) & ~early & (c + 1 < HB))
         def _():
             chunk(col - 1, c + 1)
 
-        last = dot3(split(out_ref[col + 1 + c]), (x_high[...], x_low[...]))
+        last = dot3(split(work[col + 1 + c]), (x_high[...], x_low[...]))
 
         @pl.when(col < ncol - 1)
         def _():
@@ -356,14 +396,16 @@
 
         @pl.when(col == ncol - 1)
         def _():
-            out_ref[col + 1 + c] = last
+            work[col + 1 + c] = last
+            row_out(col + 1 + c).start()
 
     store_swapped(col)
 
     def permute(c):
         parts = split3(mult[col, c])
         target = f_high[...]
-        out_ref[col + 1 + c] = dot(parts[0], target) + (dot(parts[1], target) + dot(parts[2], target))
+        work[col + 1 + c] = dot(parts[0], target) + (dot(parts[1], target) + dot(parts[2], target))
+        row_out(col + 1 + c).start()
 
     permute(0)
 
@@ -382,7 +424,11 @@
             def _(c):
                 forward(col, c, start, near=False, x=c >= sent_x, y=c >= middle)
 
-    lax.fori_loop(jnp.where(early, jnp.maximum(first, col - 1), first), col + 1, drain, 0)
+    lax.fori_loop(jnp.where(final, jnp.maximum(first, col - 1), first), col + 1, drain, 0)
+
+    @pl.loop(0, work.shape[0])
+    def _(r):
+        row_out(r).wait()
 
 
 def local(matrix, pivots, seeds):
@@ -397,8 +443,9 @@
         functools.partial(kernel, ncol, nrow),
         out_shape=jax.ShapeDtypeStruct(matrix.shape, F32),
         in_specs=[pl.BlockSpec(memory_space=pl.ANY), vmem, vmem],
-        out_specs=vmem,
+        out_specs=pl.BlockSpec(memory_space=pl.ANY),
         scratch_shapes=[
+            pltpu.VMEM(matrix.shape, F32),
             pltpu.VMEM((ncol, nrow, share, width), F32),
             pltpu.VMEM((ncol, HB, share, width), F32),
             pltpu.VMEM((ncol, width, width), BF16),
@@ -417,6 +464,7 @@
             pltpu.SemaphoreType.DMA,
             pltpu.SemaphoreType.REGULAR,
             pltpu.SemaphoreType.REGULAR,
+            pltpu.SemaphoreType.DMA((nblk,)),
         ],
         compiler_params=pltpu.CompilerParams(
             collective_id=0, has_side_effects=True, vmem_limit_bytes=limit

time: 195 us -> 190 us (0.974)
  Pallas kernels: 191 us -> 186 us
    pallas_call x1, Pallas kernels: 191 us -> 186 us  [local(): pl.pallas_call(functools.partial(kernel, ncol, nrow), out_shape=jax.Shape...]
where the time goes in v3:
time: 190 us
  Pallas kernels  186 us (98%)
  local copies, waits for them, and re-layouts  3.96 us (2%)
    pallas_call x1, Pallas kernels, local(): pl.pallas_call(functools.partial(kernel, ncol, nrow), out_shape=jax.Shape...  186 us
    unnamed x5, local copies, waits for them, and re-layouts  3.96 us

profile of v3, /device:TPU:7, one launch (start us, length us, event | category | flops | bytes accessed | tf_op | source)
XLA Modules:
  0.0 189.9 jit_solution(16494368177344955476)
XLA Ops:
  0.0 0.0 copy-start
  0.0 1.2 copy-done
  1.2 0.0 copy-start.1
  1.2 0.7 copy-done.1
  1.9 186.0 %shard_map.37 = f32[16,128,512]{2,1,0:T(8,128)S(1)} custom-call(f32[16,128,512]{2,1,0:T(8,128)} %a_hbm.1, s32[8,512]{1,0:T(8,128)S(1)} %copy-done.1, f32[1,512,512]{2,1,0:T(8,128)S(1)} %copy-done), custom_call_target="tpu_custom_call" | custom-call | tf_op jit(solution)/shard_map/pallas_call | solution.py:442
  187.9 2.0 %copy.5 = f32[16,128,512]{2,1,0:T(8,128)} copy(f32[16,128,512]{2,1,0:T(8,128)S(1)} %shard_map.37) | data formatting | bytes 8388608
Async XLA Ops:
  0.0 1.2 copy-start
  1.2 0.7 copy-start.1

commit v4 on v3

--- a/solution.py
+++ b/solution.py
@@ -34,8 +34,8 @@
 
 
 def kernel(
-    ncol, nrow, a_hbm, piv_ref, seed_ref, out_any,
-    work, upper, mult, u_high, u_low, approx, x_high, x_low, e_high, e_low, f_high, f_low,
+    ncol, nrow, a_hbm, piv_any, seed_any, out_any,
+    piv_ref, work, upper, mult, u_high, u_low, approx, x_high, x_low, e_high, e_low, order,
     usend, urecv, msend, mrecv, lsem, turn_sem, go_sem, osem,
 ):
     square = ncol == 8 and nrow == 4 and HB >= ncol - 1
@@ -53,8 +53,11 @@
     sent_x = jnp.where(chip == 1, 2, middle)
     thin = (chip == 2) if square else (col < 0)
 
-    load = pltpu.make_async_copy(a_hbm, work, lsem)
-    load.start()
+    load = pltpu.make_async_copy(a_hbm, work, lsem.at[0])
+    load_pivots = pltpu.make_async_copy(piv_any, piv_ref, lsem.at[1])
+    load_seed = pltpu.make_async_copy(seed_any.at[0], approx, lsem.at[2])
+    for copy in (load, load_pivots, load_seed):
+        copy.start()
     barrier = pltpu.get_barrier_semaphore()
     for step in range(1, nrow):
         pl.semaphore_signal(
@@ -243,8 +246,11 @@
 
     start_gather(first)
 
+    load_pivots.wait()
     scatter = one_hot(col)
-    seed_parts = split3(seed_ref[0])
+    order[...] = scatter
+    load_seed.wait()
+    seed_parts = split3(approx[...])
     contract = (((1,), (1,)), ((), ()))
     total = lax.dot_general(seed_parts[2], scatter, contract, preferred_element_type=F32)
     total += lax.dot_general(seed_parts[1], scatter, contract, preferred_element_type=F32)
@@ -325,7 +331,7 @@
         lax.fori_loop(first, col - 1, drain, 0)
 
     seed = (x_high[...], x_low[...])
-    product = dot3(split(work[col + 1]), seed)
+    mult[col, 0] = dot3(split(work[col + 1]), seed)
 
     def residual(source):
         high, low = split(upper[col, source])
@@ -344,9 +350,14 @@
         wait_share(col, source)
         residual(source)
     error = (e_high[...].reshape(width, width), e_low[...].reshape(width, width))
-    product = product + dot3(split(product), error)
-    mult[col, 0] = product + dot3(split(dot3(split(product), error)), error)
-    forward(col, 0, start)
+
+    @pl.when(col < ncol - 1)
+    def _():
+        product = mult[col, 0]
+        product = product + dot3(split(product), error)
+        mult[col, 0] = product + dot3(split(dot3(split(product), error)), error)
+        forward(col, 0, start)
+
     if square:
         @pl.when(core == 1)
         def _():
@@ -356,23 +367,19 @@
     better = approx[...] + dot3((x_high[...], x_low[...]), error)
     better = better + dot3(split(better), split(dot3(error, error)))
 
-    target = one_hot(col)
-    f_high[...] = target
+    high, low = split(better)
 
     @pl.when(col == ncol - 1)
     def _():
-        parts = split3(better)
-        swapped = dot(parts[0], target) + (dot(parts[1], target) + dot(parts[2], target))
-        high, low = split(swapped)
+        target = order[...]
+        x_high[...] = dot(high, target).astype(BF16)
+        x_low[...] = dot(low, target).astype(BF16)
+
+    @pl.when(col < ncol - 1)
+    def _():
         x_high[...] = high
         x_low[...] = low
 
-    @pl.when(col < ncol - 1)
-    def _():
-        high, low = split(better)
-        x_high[...] = high
-        x_low[...] = low
-
     @pl.when(~early)
     def _():
         rest(col - 2)
@@ -381,9 +388,9 @@
     def _():
         overdue(1)
 
-    @pl.loop(1, HB)
+    @pl.loop(jnp.where(col < ncol - 1, 1, 0), HB)
     def _(c):
-        @pl.when((col > first) & ~early & (c + 1 < HB))
+        @pl.when((col > first) & ~early & (c > 0) & (c + 1 < HB))
         def _():
             chunk(col - 1, c + 1)
 
@@ -403,15 +410,13 @@
 
     def permute(c):
         parts = split3(mult[col, c])
-        target = f_high[...]
+        target = order[...]
         work[col + 1 + c] = dot(parts[0], target) + (dot(parts[1], target) + dot(parts[2], target))
         row_out(col + 1 + c).start()
 
-    permute(0)
-
     @pl.when(col < ncol - 1)
     def _():
-        @pl.loop(1, HB)
+        @pl.loop(0, HB)
         def _(c):
             permute(c)
 
@@ -435,16 +440,17 @@
     ncol = lax.axis_size("col")
     nrow = lax.axis_size("row")
     nblk, share, width = matrix.shape
-    vmem = pl.BlockSpec(memory_space=pltpu.VMEM)
+    anywhere = pl.BlockSpec(memory_space=pl.ANY)
     half = pltpu.VMEM((width, width), BF16)
     words = 2 * nblk * share * width + ncol * width * width * 2 + ncol * HB * share * width + 6 * width * width
     limit = min(4 * words + 2**20, 60 * 1024 * 1024)
     return pl.pallas_call(
         functools.partial(kernel, ncol, nrow),
         out_shape=jax.ShapeDtypeStruct(matrix.shape, F32),
-        in_specs=[pl.BlockSpec(memory_space=pl.ANY), vmem, vmem],
-        out_specs=pl.BlockSpec(memory_space=pl.ANY),
+        in_specs=[anywhere] * 3,
+        out_specs=anywhere,
         scratch_shapes=[
+            pltpu.VMEM(pivots.shape, jnp.int32),
             pltpu.VMEM(matrix.shape, F32),
             pltpu.VMEM((ncol, nrow, share, width), F32),
             pltpu.VMEM((ncol, HB, share, width), F32),
@@ -456,12 +462,11 @@
             pltpu.VMEM((nrow, share, width), BF16),
             pltpu.VMEM((nrow, share, width), BF16),
             half,
-            half,
             pltpu.SemaphoreType.DMA((ncol, nrow)),
             pltpu.SemaphoreType.DMA((ncol, nrow)),
             pltpu.SemaphoreType.DMA((ncol, HB, 3)),
             pltpu.SemaphoreType.DMA((ncol, HB)),
-            pltpu.SemaphoreType.DMA,
+            pltpu.SemaphoreType.DMA((3,)),
             pltpu.SemaphoreType.REGULAR,
             pltpu.SemaphoreType.REGULAR,
             pltpu.SemaphoreType.DMA((nblk,)),

time: 190 us -> 189 us (level)
  no operation moved by 1% of the time
where the time goes in v4:
time: 189 us
  Pallas kernels  185 us (98%)
  local copies, waits for them, and re-layouts  3.96 us (2%)
    pallas_call x1, Pallas kernels, local(): pl.pallas_call(functools.partial(kernel, ncol, nrow), out_shape=jax.Shape...  185 us
    unnamed x5, local copies, waits for them, and re-layouts  3.96 us

profile of v4, /device:TPU:7, one launch (start us, length us, event | category | flops | bytes accessed | tf_op | source)
XLA Modules:
  0.0 189.1 jit_solution(2635095637881180236)
XLA Ops:
  0.0 0.0 copy-start
  0.0 1.2 copy-done
  1.2 0.0 copy-start.1
  1.2 0.7 copy-done.1
  1.9 185.1 %shard_map.37 = f32[16,128,512]{2,1,0:T(8,128)S(1)} custom-call(f32[16,128,512]{2,1,0:T(8,128)} %a_hbm.1, s32[8,512]{1,0:T(8,128)S(1)} %copy-done.1, f32[1,512,512]{2,1,0:T(8,128)S(1)} %copy-done), custom_call_target="tpu_custom_call" | custom-call | tf_op jit(solution)/shard_map/pallas_call | solution.py:447
  187.1 2.0 %copy.5 = f32[16,128,512]{2,1,0:T(8,128)} copy(f32[16,128,512]{2,1,0:T(8,128)S(1)} %shard_map.37) | data formatting | bytes 8388608
Async XLA Ops:
  0.0 1.2 copy-start
  1.2 0.7 copy-start.1

commit v5 on v4

--- a/solution.py
+++ b/solution.py
@@ -50,7 +50,7 @@
 
     middle = HB // 2 + 1
     holds = (core == 0) if square else (col < 0)
-    sent_x = jnp.where(chip == 1, 2, middle)
+    sent_x = jnp.where(chip == 1, 3, middle)
     thin = (chip == 2) if square else (col < 0)
 
     load = pltpu.make_async_copy(a_hbm, work, lsem.at[0])

time: 189 us -> 189 us (level)
  no operation moved by 1% of the time
where the time goes in v5:
time: 189 us
  Pallas kernels  185 us (98%)
  local copies, waits for them, and re-layouts  3.96 us (2%)
    pallas_call x1, Pallas kernels, local(): pl.pallas_call(functools.partial(kernel, ncol, nrow), out_shape=jax.Shape...  185 us
    unnamed x5, local copies, waits for them, and re-layouts  3.96 us

profile of v5, /device:TPU:7, one launch (start us, length us, event | category | flops | bytes accessed | tf_op | source)
XLA Modules:
  0.0 189.1 jit_solution(13153263719751467547)
XLA Ops:
  0.0 0.0 copy-start
  0.0 1.2 copy-done
  1.2 0.0 copy-start.1
  1.2 0.7 copy-done.1
  1.9 185.2 %shard_map.37 = f32[16,128,512]{2,1,0:T(8,128)S(1)} custom-call(f32[16,128,512]{2,1,0:T(8,128)} %a_hbm.1, s32[8,512]{1,0:T(8,128)S(1)} %copy-done.1, f32[1,512,512]{2,1,0:T(8,128)S(1)} %copy-done), custom_call_target="tpu_custom_call" | custom-call | tf_op jit(solution)/shard_map/pallas_call | solution.py:447
  187.1 2.0 %copy.5 = f32[16,128,512]{2,1,0:T(8,128)} copy(f32[16,128,512]{2,1,0:T(8,128)S(1)} %shard_map.37) | data formatting | bytes 8388608
Async XLA Ops:
  0.0 1.2 copy-start
  1.2 0.7 copy-start.1
